TPU v7x, 32 devices: a whole 2x2x4 slice. The times are simulated.
32 devices in a mesh: ctx: 16 (over z, x, core), mp: 2 (over y).
Axes of the slice: x: 2, y: 2, z: 4, core: 2. Of those that a mesh axis runs over, the one named last changes fastest.
Arguments:
- query_proj: bfloat16 [2048, 4096], P(('ctx', 'mp')), may hold values from -91.92388 to 91.92388
- keyval_proj: bfloat16 [2048, 8, 256], P(('ctx', 'mp')), may hold values from -12 to 12
- hidden: bfloat16 [2048, 4096], P('ctx', 'mp'), may hold values from -6 to 6
- weight_x: bfloat16 [4096, 1024], P(None, 'mp'), may hold values from -0.09375 to 0.09375
- conv_x: float32 [4, 1024], P(None, 'mp'), may hold values from -3 to 3
- conv_b: float32 [4, 1024], P(None, 'mp'), may hold values from -3 to 3
- conv_c: float32 [4, 4096], P(None, 'mp'), may hold values from -3 to 3
- step_size: float32 [2048, 32], P('ctx', 'mp'), may hold values from 0 to 1.2, as said below
- decay_log: float32 [32], P('mp'), may hold values from -0.5 to 0.5
- skip_gain: float32 [32], P('mp'), may hold values from 0.5 to 1.5
Outputs:
- student_out: bfloat16 [2048, 4096], P('ctx', 'mp')
- weight_grad: float32 [4096, 1024], P('ctx', 'mp')
Inputs may be any that keep to these rules, and one draw needn't show every extreme that they name: `step_size`: positive.
All inputs are finite; a program needn't handle non-finite values.
Results may differ from a plain program's by a relative error of at most 0.001.
The roundings to bfloat16 on the way count: a program that leaves them out, or rounds other values in their place, can miss the bound.
Values may be sent and summed in bfloat16 or wider, within the bound.
No kernel may reach another device: no remote copies, remote signals or barrier semaphores. Data moves between devices by JAX's collectives and lax.ppermute only.
A program may use at most 128 MiB of HBM per device.

v0:
```python
import jax
import jax.numpy as jnp
from jax import lax
from jax.sharding import PartitionSpec as P

HEAD_TOTAL = 32
KV = 8
HD = 128
CONV = 4


highest_precision = lax.Precision.HIGHEST
negative = -1e30


def shifted(value, axis, steps):
    count = lax.axis_size(axis)
    leading, last = (max(0, -steps), min(count, count - steps))
    return lax.ppermute(value, axis, [(source, source + steps) for source in range(leading, last)])


def carried_in(value, axis, join, neutral, backward):
    count, mine = (lax.axis_size(axis), lax.axis_index(axis))
    pieces = jax.tree.map(lambda part: lax.all_gather(part, axis), value)
    if backward:
        pieces = jax.tree.map(lambda part: part[::-1], pieces)
        mine = count - 1 - mine
    subtotal = jax.tree.map(
        lambda part, zero: jnp.full_like(part, 0) + jnp.asarray(zero, part.dtype), value, neutral
    )

    def lap(position, subtotal):
        longer = join(subtotal, jax.tree.map(lambda part: part[position], pieces))
        return jax.tree.map(lambda new, old: jnp.where(position < mine, new, old), longer, subtotal)

    return lax.fori_loop(0, count - 1, lap, subtotal)


def causal_conv(head_rows, signal, kernel):
    length = signal.shape[0]
    extended = jnp.concatenate([head_rows, signal], axis=0).astype(jnp.float32)
    result = jnp.zeros((length, signal.shape[1]), jnp.float32)
    for offset in range(CONV):
        result = result + kernel[offset][None, :] * extended[offset : offset + length]
    return result


def chain_combine(earlier, later):
    return (earlier[0] * later[0], later[0][..., None, None] * earlier[1] + later[1])


def local(
    query_proj,
    keyval_proj,
    hidden,
    weight_x,
    conv_x,
    conv_b,
    conv_c,
    step_size,
    decay_log,
    skip_gain,
):
    groups = KV // lax.axis_size("mp")
    per_group = HEAD_TOTAL // KV
    group_width = per_group * HD
    raw_count = query_proj.shape[0]
    query_grouped = query_proj.reshape(raw_count, KV, group_width)
    query_local, keyval_local = (
        lax.all_to_all(query_grouped, "mp", split_axis=1, concat_axis=0, tiled=True),
        lax.all_to_all(keyval_proj, "mp", split_axis=1, concat_axis=0, tiled=True),
    )
    row_count = query_local.shape[0]
    shard_index = lax.axis_index("ctx")
    first_row = shard_index * row_count
    row_positions = first_row + jnp.arange(row_count, dtype=jnp.int32)
    query_total = per_group * row_count
    query_heads = jnp.transpose(
        query_local.reshape(row_count, groups, per_group, HD), (1, 2, 0, 3)
    ).reshape(groups, query_total, HD)
    query_pos = jnp.tile(row_positions, per_group)
    last_query = jnp.max(row_positions)
    score_scale = HD ** (-0.5)

    def attend_all(state_carry, shard_piece):
        piece_rows = shard_piece.shape[0]
        block_size = 512
        block_count = piece_rows // block_size
        blocks = shard_piece.reshape(block_count, block_size, groups, 2 * HD)

        def one_block(inner_carry, block_index):
            row_max, norm_total, weighted = inner_carry
            key_block = lax.dynamic_index_in_dim(blocks, block_index, 0, keepdims=False)
            scores = (
                jnp.einsum(
                    "gqd,kgd->gqk",
                    query_heads,
                    key_block[:, :, :HD],
                    preferred_element_type=jnp.float32,
                )
                * score_scale
            )
            key_pos = block_index * block_size + jnp.arange(block_size, dtype=jnp.int32)
            allowed = (key_pos[None, :] <= query_pos[:, None])[None]
            scores = jnp.where(allowed, scores, negative)
            new_max = jnp.maximum(row_max, jnp.max(scores, axis=2))
            weights = jnp.where(allowed, jnp.exp(scores - new_max[:, :, None]), 0.0)
            factor = jnp.exp(row_max - new_max)
            norm_total = norm_total * factor + jnp.sum(weights, axis=2)
            mixed = jnp.einsum(
                "gqk,kgd->gqd",
                weights.astype(jnp.bfloat16),
                key_block[:, :, HD:],
                preferred_element_type=jnp.float32,
            )
            weighted = weighted * factor[:, :, None] + mixed
            return ((new_max, norm_total, weighted), None)

        result, unused = lax.scan(one_block, state_carry, jnp.arange(block_count, dtype=jnp.int32))
        return result

    start_carry = (
        jnp.full((groups, query_total), negative, jnp.float32),
        jnp.zeros((groups, query_total), jnp.float32),
        jnp.zeros((groups, query_total, HD), jnp.float32),
    )
    shard_piece = lax.all_gather(keyval_local, "ctx", axis=0, tiled=True)
    row_max, norm_total, weighted = lax.cond(
        jnp.int32(0) > last_query,
        lambda kept: kept,
        lambda kept: attend_all(kept, shard_piece),
        start_carry,
    )
    target = jnp.transpose(
        (weighted / norm_total[..., None]).reshape(groups, per_group, row_count, HD), (2, 0, 1, 3)
    )
    x_input = jnp.dot(
        lax.all_gather(hidden, "mp", axis=1, tiled=True),
        weight_x,
        preferred_element_type=jnp.float32,
    ).astype(jnp.bfloat16)
    rim_width = CONV - 1
    x_width = groups * HD
    key_rows = keyval_local[:, :, :HD].reshape(row_count, x_width)
    query_rows = query_local.reshape(row_count, groups * group_width)
    tail_rows = jnp.concatenate(
        [x_input[-rim_width:], key_rows[-rim_width:], query_rows[-rim_width:]], axis=1
    )
    before = shifted(tail_rows, "ctx", 1)
    x_pre = causal_conv(before[:, :x_width], x_input, conv_x)
    x_conv = jax.nn.silu(x_pre)
    b_conv = jax.nn.silu(causal_conv(before[:, x_width : 2 * x_width], key_rows, conv_b))
    c_conv = jax.nn.silu(causal_conv(before[:, 2 * x_width :], query_rows, conv_c))
    x_groups = x_conv.reshape(row_count, groups, HD)
    input_proj_groups = b_conv.reshape(row_count, groups, HD)
    readout_heads = c_conv.reshape(row_count, groups, per_group, HD)
    step_heads = step_size.reshape(row_count, groups, per_group)
    decay_rate = -jnp.exp(decay_log).reshape(groups, per_group)
    skip_heads = skip_gain.reshape(groups, per_group)
    log_decay = jnp.cumsum(step_heads * decay_rate[None], axis=0)
    ordered = jnp.transpose(log_decay, (1, 2, 0))
    causal = jnp.arange(row_count)[:, None] >= jnp.arange(row_count)[None, :]
    differ = ordered[:, :, :, None] - ordered[:, :, None, :]
    within = jnp.where(causal, jnp.exp(jnp.where(causal, differ, 0.0)), 0.0)
    pairwise_scores = jnp.einsum(
        "qmzo,imo->mzqi", readout_heads, input_proj_groups, precision=highest_precision
    )
    mixing_weights = pairwise_scores * within
    driven_state = step_heads[..., None] * x_groups[:, :, None, :]
    inner_portion = jnp.einsum(
        "hewl,lhen->when", mixing_weights, driven_state, precision=highest_precision
    )
    to_end = jnp.exp(log_decay[-1][None] - log_decay)
    local_state = jnp.einsum(
        "sgn,sgrp->grnp",
        input_proj_groups,
        to_end[..., None] * driven_state,
        precision=highest_precision,
    )
    block_decay = jnp.exp(log_decay[-1])
    identity = (jnp.ones_like(block_decay), jnp.zeros_like(local_state))
    chained = carried_in((block_decay, local_state), "ctx", chain_combine, identity, False)
    incoming = chained[1]
    growth = jnp.exp(log_decay)
    carried = growth[..., None] * jnp.einsum(
        "tgrn,grnp->tgrp", readout_heads, incoming, precision=highest_precision
    )
    student = inner_portion + carried + skip_heads[None, :, :, None] * x_groups[:, :, None, :]
    upstream_gradient = 2.0 * (student - target) / (HEAD_TOTAL * HD)
    state_grad = jnp.einsum(
        "tgrn,tgrp->grnp",
        growth[..., None] * readout_heads,
        upstream_gradient,
        precision=highest_precision,
    )
    reverse = carried_in((block_decay, state_grad), "ctx", chain_combine, identity, True)
    later_grad = reverse[1]
    inner_backward = jnp.einsum(
        "lvyq,ylve->qlve", mixing_weights, upstream_gradient, precision=highest_precision
    )
    back_state = to_end[..., None] * jnp.einsum(
        "sgn,grnp->sgrp", input_proj_groups, later_grad, precision=highest_precision
    )
    head_grad = (
        step_heads[..., None] * (inner_backward + back_state)
        + skip_heads[None, :, :, None] * upstream_gradient
    )
    x_grad = jnp.sum(head_grad, axis=2).reshape(row_count, x_width)
    sigmoid_x = jax.nn.sigmoid(x_pre)
    pre_grad = x_grad * sigmoid_x * (1.0 + x_pre * (1.0 - sigmoid_x))
    after = shifted(pre_grad[:rim_width], "ctx", -1)
    extended = jnp.concatenate([pre_grad, after], axis=0)
    input_grad = jnp.zeros_like(pre_grad)
    for offset in range(CONV):
        input_grad = (
            input_grad
            + conv_x[offset][None, :] * extended[CONV - 1 - offset : CONV - 1 - offset + row_count]
        )
    input_rounded = input_grad.astype(jnp.bfloat16)
    hidden_whole = lax.all_gather(hidden, "mp", axis=1, tiled=True)
    weight_grad = lax.psum_scatter(
        lax.dot_general(
            hidden_whole,
            input_rounded,
            (((0,), (0,)), ((), ())),
            preferred_element_type=jnp.float32,
        ),
        "ctx",
        scatter_dimension=0,
        tiled=True,
    )
    student_out = student.reshape(row_count, groups * group_width).astype(jnp.bfloat16)
    return (student_out, weight_grad)


def solution(mesh):
    return jax.shard_map(
        local,
        mesh=mesh,
        in_specs=(
            P(("ctx", "mp"), None),
            P(("ctx", "mp"), None, None),
            P("ctx", "mp"),
            P(None, "mp"),
            P(None, "mp"),
            P(None, "mp"),
            P(None, "mp"),
            P("ctx", "mp"),
            P("mp"),
            P("mp"),
        ),
        out_specs=(P("ctx", "mp"), P("ctx", "mp")),
        check_vma=False,
    )
```

profile of v0, /device:TPU:0, one launch (start us, length us, event | category | flops | bytes accessed | tf_op | source)
XLA Modules:
  0.0 536.4 jit_solution(11572900788076267873)
XLA Ops:
  9.0 9.2 %all_to_all.33 = bf16[64,8,256]{2,0,1:T(8,128)(2,1)S(1)} all-to-all(bf16[64,8,256]{2,0,1:T(8,128)(2,1)S(1)} %copy.93), channel_id=1, replica_groups=mesh['ctx'=16,'mp'=2] {'mp'}, dimensions={1} | all-to-all | bytes 524288 | tf_op jit(solution)/shard_map/all_to_all | solution.py:71
  20.9 3.5 all-to-all-start.1
  25.2 13.4 %all-to-all-done.1 = bf16[64,8,512]{2,0,1:T(8,128)(2,1)S(1)} async-done(((bf16[64,8,512]{2,0,1:T(8,128)(2,1)}), bf16[64,8,512]{2,0,1:T(8,128)(2,1)S(1)}, u32[]{:S(2)}, u32[]{:S(2)}) %all-to-all-start.1) | async-done | bytes 524320 | tf_op jit(solution)/shard_map/all_to_all | solution.py:70
  50.5 24.6 %all_gather.26 = f32[16,4,4]{2,1,0:T(4,128)S(1)} all-gather(f32[1,4,4]{2,1,0:T(4,128)S(1)} %get-tuple-element.426), channel_id=1, replica_groups=mesh['ctx'=16,'mp'=2] {'ctx'}, dimensions={0}, use_global_device_ids=true | all-gather | bytes 1088 | tf_op jit(solution)/shard_map/all_gather | solution.py:24
  79.3 13.2 %all-gather.9.cloned.1.call-done = bf16[2048,4,256]{2,0,1:T(8,128)(2,1)} async-done(((bf16[128,4,256]{2,0,1:T(8,128)(2,1)}), bf16[2048,4,256]{2,0,1:T(8,128)(2,1)}) %all-gather.9.cloned.1.call-update) | async-done | bytes 4194320 | tf_op jit(solution)/shard_map/all_gather | solution.py:127
  92.5 63.4 %conditional.1 = (f32[4,512]{1,0:T(4,128)S(1)}, f32[4,512,128]{2,1,0:T(8,128)}) conditional(s32[]{:T(128)} %convert_element_type.33, (bf16[2048,4,256]{2,0,1:T(8,128)(2,1)}, bf16[4,4,128,128]{3,1,2,0:T(4,128)(2,1)}, s32[]{:T(128)}, s32[1,128]{1,0:T(1,128)S(1)}) %tuple.146, () %tuple.50), branch_computations={%region_4.9_spmd, %region_9.10_spmd} | conditional | flops 551561856 | bytes 37365608 | solution.py:128
  94.4 61.5 %while.42 = (s32[]{:T(128)}, f32[4,512]{1,0:T(4,128)S(1)}, f32[4,512]{1,0:T(4,128)S(1)}, f32[4,512,128]{2,1,0:T(8,128)}, s32[4]{0:T(128)S(1)}, /*index=5*/bf16[4...) while((s32[]{:T(128)}, f32[4,512]{1,0:T(4,128)S(1)}, ...), condition=%wide.region_8.8_spmd.clone, body=%wide.region_5.7_spmd.clone.sunk | while | flops 551561728 | bytes 36315868 | solution.py:119
  99.1 3.9 fusion.114
  103.0 3.4 fusion.115
  113.6 3.9 fusion.114
  117.6 3.4 fusion.115
  121.0 3.6 fusion.117
  129.2 3.9 fusion.114
  136.6 3.6 fusion.117
  144.8 4.1 fusion.114
  152.4 3.6 fusion.117
  158.8 60.8 %all-gather.11.cloned.1.call-done = f32[64,4,128,128]{3,2,1,0:T(8,128)} async-done(((f32[4,4,128,128]{3,2,1,0:T(8,128)}), f32[64,4,128,128]{3,2,1,0:T(8,128)}) %all-gather.11.cloned.1.call-update) | async-done | bytes 16777232 | tf_op jit(solution)/shard_map/all_gather | solution.py:24
  219.6 22.5 %while.43 = (s32[]{:T(128)}, f32[4,4,128,128]{3,2,1,0:T(8,128)S(1)}, s32[]{:T(128)}, f32[16,4,4]{2,1,0:T(4,128)S(1)}, f32[16,4,4,128,128]{4,3,2,1,0:T(8,128)}, /*index=5*/s32[]{:T(128)}, s32[]{:T(128)}) while((s32[]{:T(128)}, f32[4,4,128,128]{3,2,1,0:T(8,128)S(1)}, s32[]{:T(128)}, f32[16,4,4]{2,1,0:T(4,128)S(1)}, ...), condition=%wide.region_2.3_spmd.clone, body=%wide.region_1.2_spmd.clone.sunk | while | flops 1048580 | bytes 3146025 | solution.py:36
  249.5 124.7 %all-gather.13.cloned.1.call-done = f32[64,4,128,128]{3,2,1,0:T(8,128)} async-done(((f32[4,4,128,128]{3,2,1,0:T(8,128)}), f32[64,4,128,128]{3,2,1,0:T(8,128)}) %all-gather.13.cloned.1.call-update) | async-done | bytes 16777232 | tf_op jit(solution)/shard_map/all_gather | solution.py:24
  374.2 11.6 %rev.7 = f32[16,4,4,128,128]{4,3,2,1,0:T(8,128)} reverse(f32[16,4,4,128,128]{4,3,2,1,0:T(8,128)} %bitcast.167), dimensions={0} | reverse | bytes 33554432 | tf_op jit(solution)/shard_map/rev | solution.py:26
  385.9 22.5 %while.44 = (s32[]{:T(128)}, f32[4,4,128,128]{3,2,1,0:T(8,128)S(1)}, s32[]{:T(128)}, f32[16,4,4]{2,1,0:T(4,128)S(1)}, f32[16,4,4,128,128]{4,3,2,1,0:T(8,128)}, /*index=5*/s32[]{:T(128)}, s32[]{:T(128)}) while((s32[]{:T(128)}, f32[4,4,128,128]{3,2,1,0:T(8,128)S(1)}, s32[]{:T(128)}, f32[16,4,4]{2,1,0:T(4,128)S(1)}, ...), condition=%wide.region_11.12_spmd.clone, body=%wide.region_10.11_spmd.clone.sunk | while | flops 1048580 | bytes 3146025 | solution.py:36
  410.3 4.0 fusion.37
  418.5 4.6 convolution_bitcast_fusion
  425.2 102.6 %reduce-scatter.2.cloned.1.call-done = f32[256,512]{0,1:T(8,128)} async-done(((f32[4096,512]{0,1:T(8,128)}), f32[256,512]{0,1:T(8,128)}) %reduce-scatter.2.cloned.1.call-update) | async-done | bytes 524304 | tf_op jit(solution)/shard_map/reduce_scatter | solution.py:221
  (216 shorter events, 105.0 us)
Async XLA Ops:
  7.2 17.3 %copy-start.12 = (f32[128,16]{0,1:T(8,128)S(1)}, f32[128,16]{0,1:T(8,128)}, u32[]{:S(2)}) copy-start(f32[128,16]{0,1:T(8,128)} %param.25) | copy-start | bytes 24580
  7.2 17.5 %copy-start.17 = (f32[16]{0:T(128)S(1)}, f32[16]{0:T(128)}, u32[]{:S(2)}) copy-start(f32[16]{0:T(128)} %param.26) | copy-start | bytes 196
  7.2 17.7 %copy-start.14 = (f32[4,512]{1,0:T(4,128)S(1)}, f32[4,512]{1,0:T(4,128)}, u32[]{:S(2)}) copy-start(f32[4,512]{1,0:T(4,128)} %param.22) | copy-start | bytes 24580
  7.2 17.8 %copy-start.15 = (f32[4,512]{1,0:T(4,128)S(1)}, f32[4,512]{1,0:T(4,128)}, u32[]{:S(2)}) copy-start(f32[4,512]{1,0:T(4,128)} %param.23) | copy-start | bytes 24580
  7.2 32.0 %all-gather.7.cloned.1.call-start = ((), (), s32[]{:S(2)}) async-start(), calls=%async_computation.3 | async-start | bytes 1572864 | tf_op jit(solution)/shard_map/all_gather | solution.py:138
  7.9 84.5 %all-gather.9.cloned.1.call-start = ((), (), s32[]{:S(2)}) async-start(), calls=%async_computation.4 | async-start | bytes 4456448 | tf_op jit(solution)/shard_map/all_gather | solution.py:127
  18.9 6.2 %copy-start.11 = (bf16[2,64,4,256]{3,1,0,2:T(8,128)(2,1)S(1)}, bf16[2,64,4,256]{3,1,0,2:T(8,128)(2,1)}, u32[]{:S(2)}) copy-start(bf16[2,64,4,256]{3,1,0,2:T(8,128)(2,1)} %copy.94) | copy-start | bytes 786436
  20.9 17.7 %all-to-all-start.1 = ((bf16[64,8,512]{2,0,1:T(8,128)(2,1)}), bf16[64,8,512]{2,0,1:T(8,128)(2,1)S(1)}, u32[]{:S(2)}, u32[]{:S(2)}) async-start(bf16[64,8,512]{2,0,1:T(8,128)(2,1)} %bitcast.140), calls=%async_computation.1 | async-start | bytes 1048576 | tf_op jit(solution)/shard_map/all_to_all | solution.py:70
  24.4 195.2 %all-gather.11.cloned.1.call-start = ((), (), s32[]{:S(2)}) async-start(), calls=%async_computation.6 | async-start | bytes 17825792 | tf_op jit(solution)/shard_map/all_gather | solution.py:24
  42.5 2.4 collective-permute-start
  45.9 29.2 %copy-start.13 = (f32[4,2048]{1,0:T(4,128)S(1)}, f32[4,2048]{1,0:T(4,128)}, u32[]{:S(2)}) copy-start(f32[4,2048]{1,0:T(4,128)} %param.24) | copy-start | bytes 98308
  46.0 30.1 %copy-start.8 = (f32[128,512]{0,1:T(8,128)}, f32[128,512]{0,1:T(8,128)S(1)}, u32[]{:S(2)}) copy-start(f32[128,512]{0,1:T(8,128)S(1)} %copy.131) | copy-start | bytes 786436
  46.3 30.9 %copy-start.5 = (f32[128,4,128]{2,1,0:T(4,128)}, f32[128,4,128]{2,1,0:T(4,128)S(1)}, u32[]{:S(2)}) copy-start(f32[128,4,128]{2,1,0:T(4,128)S(1)} %reshape.102) | copy-start | bytes 786436
  48.8 325.5 %all-gather.13.cloned.1.call-start = ((), (), s32[]{:S(2)}) async-start(), calls=%async_computation.7 | async-start | bytes 17825792 | tf_op jit(solution)/shard_map/all_gather | solution.py:24
  117.5 3.5 copy-start
  148.9 3.5 copy-start
  219.6 24.4 %copy-start.1 = (f32[4,4,128,128]{2,3,1,0:T(8,128)S(1)}, f32[4,4,128,128]{2,3,1,0:T(8,128)}, u32[]{:S(2)}) copy-start(f32[4,4,128,128]{2,3,1,0:T(8,128)} %fusion.31) | copy-start | bytes 3145732
  219.6 24.4 %copy-start.9 = (f32[128,512]{0,1:T(8,128)S(1)}, f32[128,512]{0,1:T(8,128)}, u32[]{:S(2)}) copy-start(f32[128,512]{0,1:T(8,128)} %copy-done.8) | copy-start | bytes 786436
  242.2 4.0 copy-start.4
  249.4 278.3 %reduce-scatter.2.cloned.1.call-start = ((), (), s32[]{:S(2)}) async-start(), calls=%async_computation.5 | async-start | bytes 8912896 | tf_op jit(solution)/shard_map/reduce_scatter | solution.py:221
  385.9 22.6 %copy-start.6 = (f32[128,4,128]{2,1,0:T(4,128)S(1)}, f32[128,4,128]{2,1,0:T(4,128)}, u32[]{:S(2)}) copy-start(f32[128,4,128]{2,1,0:T(4,128)} %copy-done.5) | copy-start | bytes 786436
  385.9 24.4 %copy-start.3 = (f32[128,4,4,128]{0,3,2,1:T(8,128)S(1)}, f32[128,4,4,128]{0,3,2,1:T(8,128)}, u32[]{:S(2)}) copy-start(f32[128,4,4,128]{0,3,2,1:T(8,128)} %copy-done.2) | copy-start | bytes 3145732
  410.3 8.3 %copy-start.7 = (bf16[128,4096]{1,0:T(8,128)(2,1)S(1)}, bf16[128,4096]{1,0:T(8,128)(2,1)}, u32[]{:S(2)}) copy-start(bf16[128,4096]{1,0:T(8,128)(2,1)} %all-gather.7.cloned.1.call-done) | copy-start | bytes 3145732
  415.5 3.1 collective-permute-start.1
  (5 other events, 14.5 us)
Sparse Core Ops, SparseCore 0:
  9.6 29.6 all-gather.6
  42.0 50.4 all-gather.8
  94.7 124.9 all-gather.10
  249.6 124.6 all-gather.12
  423.3 104.4 reduce-scatter.1
where the time goes:
time: 539 us; the launch traced here: 536 us
  waiting for transfers between devices  318 us (59%)
  other arithmetic  63.9 us (12%)
  matrix products  53.1 us (10%)
  local copies, waits for them, and re-layouts  35.1 us (7%)
  blocking collectives  33.8 us (6%)
  between operations  14.9 us (3%)
  loops' own time  11 us (2%)
  starting transfers between devices  6.56 us (1%)
    all_gather x2, waiting for transfers between devices, carried_in(): pieces = jax.tree.map(lambda part: lax.all_gather(part, axis), value)  185 us
    reduce_scatter x1, waiting for transfers between devices, local(): lax.psum_scatter(lax.dot_general(hidden_whole, input_rounded, (((0,), (0,...  103 us
    select_n x30, other arithmetic, lap(): jnp.where(position < mine, new, old)  43.9 us
    all_gather x1, blocking collectives, carried_in(): pieces = jax.tree.map(lambda part: lax.all_gather(part, axis), value)  24.6 us
    dot_general x4, matrix products, one_block(): jnp.einsum('gqd,kgd->gqk', query_heads, key_block[:, :, :HD], preferred_e...  15.9 us
    reduce_sum x4, other arithmetic, one_block(): norm_total = norm_total * factor + jnp.sum(weights, axis=2)  13.5 us
    all_to_all x1, waiting for transfers between devices, local(): lax.all_to_all(query_grouped, 'mp', split_axis=1, concat_axis=0, tiled=True)  13.4 us
    dot_general x4, matrix products, one_block(): jnp.einsum('gqk,kgd->gqd', weights.astype(jnp.bfloat16), key_block[:, :,...  13.2 us
  transfers between devices with their start and end apart: 8, of which 8 were waited for; matrix products, arithmetic and copies ran while one was open for 14% of the time, Pallas kernels for 0%

commit v1 on v0

--- a/solution.py
+++ b/solution.py
@@ -1,6 +1,9 @@
 import jax
 import jax.numpy as jnp
 from jax import lax
+from jax.experimental import pallas as pl
+from jax.experimental.pallas import tpu as pltpu
+from jax.sharding import Mesh
 from jax.sharding import PartitionSpec as P
 
 HEAD_TOTAL = 32
@@ -49,7 +52,7 @@
     return (earlier[0] * later[0], later[0][..., None, None] * earlier[1] + later[1])
 
 
-def local(
+def sequence_local(
     query_proj,
     keyval_proj,
     hidden,
@@ -233,22 +236,324 @@
     return (student_out, weight_grad)
 
 
+CHUNK = 256
+SWAP = ((0, 1), (1, 0))
+bf16, f32 = jnp.bfloat16, jnp.float32
+NT = (((1,), (1,)), ((), ()))
+TN = (((0,), (0,)), ((), ()))
+NN = (((1,), (0,)), ((), ()))
+VMEM_BLOCK = pl.BlockSpec(memory_space=pltpu.VMEM)
+SMEM_BLOCK = pl.BlockSpec(memory_space=pltpu.SMEM)
+PARAMS = pltpu.CompilerParams(vmem_limit_bytes=56 * 1024 * 1024)
+
+
+def swap(value, axis):
+    return lax.ppermute(value, axis, SWAP)
+
+
+def split(value):
+    high = value.astype(bf16)
+    return high, (value - high.astype(f32)).astype(bf16)
+
+
+def dot3(left, right, dims):
+    (left_axis,), (right_axis,) = dims[0]
+    lh, ll = split(left)
+    rh, rl = split(right)
+    return lax.dot_general(
+        jnp.concatenate([lh, ll, lh], axis=left_axis),
+        jnp.concatenate([rh, rh, rl], axis=right_axis),
+        dims,
+        preferred_element_type=f32,
+    )
+
+
+def rows(index, size):
+    return pl.ds(pl.multiple_of(index * size, size), size)
+
+
+def attend_kernel(where_ref, q_ref, *refs):
+    kv_refs, (out_ref, kv_all) = refs[:4], refs[4:]
+    tokens = q_ref.shape[0]
+    place = where_ref[1]
+    block = tokens // 16
+    for delta in range(4):
+        for z in range(4):
+            kv_all[rows(z * 4 + (place ^ delta), block), :] = kv_refs[delta][z * block : (z + 1) * block, :]
+    scale = HD ** (-0.5)
+    diag = lax.broadcasted_iota(jnp.int32, (CHUNK, CHUNK), 0) >= lax.broadcasted_iota(
+        jnp.int32, (CHUNK, CHUNK), 1
+    )
+    for i in range(tokens // CHUNK):
+        q = q_ref[i * CHUNK : (i + 1) * CHUNK, :]
+        last = lax.dot_general(
+            q, kv_all[i * CHUNK : (i + 1) * CHUNK, :HD], NT, preferred_element_type=f32
+        )
+        last = jnp.where(diag, last, negative)
+        if i:
+            score = lax.dot_general(q, kv_all[: i * CHUNK, :HD], NT, preferred_element_type=f32)
+            score = jnp.concatenate([score, last], axis=1)
+        else:
+            score = last
+        top = jnp.max(score, axis=1, keepdims=True)
+        weight = jnp.exp((score - top) * scale)
+        total = jnp.sum(weight, axis=1, keepdims=True)
+        mixed = lax.dot_general(
+            weight.astype(bf16), kv_all[: (i + 1) * CHUNK, HD:], NN, preferred_element_type=f32
+        )
+        out_ref[i * CHUNK : (i + 1) * CHUNK, :] = mixed / total
+
+
+def silu(value):
+    return value / (1.0 + jnp.exp(-value))
+
+
+def student_kernel(where_ref, rate_ref, skip_ref, q_ref, target_ref, conv_x_ref, conv_b_ref, conv_c_ref, *refs):
+    kv_refs, x_refs = refs[:4], refs[4:8]
+    y_ref, grad_ref = refs[8:10]
+    x_pad, b_pad, c_pad, b_all, c_all, slope_all, y_all, dt_all = refs[10:]
+    tokens = q_ref.shape[0]
+    count = tokens // CHUNK
+    block = tokens // 16
+    z_mine, place, head = where_ref[0], where_ref[1], where_ref[2]
+    rim = 8
+    for pad in (x_pad, b_pad, c_pad):
+        pad[0:rim, :] = jnp.zeros((rim, HD), f32)
+    mine = lax.broadcasted_iota(jnp.int32, (16, HD), 0) % 4 == place
+    for delta in range(4):
+        for z in range(4):
+            index = z * 4 + (place ^ delta)
+            at = pl.ds(pl.multiple_of(rim + index * block, 8), block)
+            x_pad[at, :] = x_refs[delta][z, :block, :].astype(f32)
+            b_pad[at, :] = kv_refs[delta][z * block : (z + 1) * block, :HD].astype(f32)
+            pieces = x_refs[delta][z, block : block + 16, :].astype(f32)
+            step = jnp.sum(jnp.where(mine, pieces, 0.0), axis=0, keepdims=True)
+            dt_all[rows(index, 8), :] = jnp.broadcast_to(step, (8, HD))
+    c_pad[rim : rim + tokens, :] = q_ref[...].astype(f32)
+    taps_x = conv_x_ref[:, pl.ds(pl.multiple_of(z_mine * HD, HD), HD)]
+    taps_b = conv_b_ref[:, pl.ds(pl.multiple_of(z_mine * HD, HD), HD)]
+    taps_c = conv_c_ref[:, pl.ds(pl.multiple_of(head * HD, HD), HD)]
+    rate = -jnp.exp(jnp.full((1, HD), rate_ref[head], f32))[:, :1]
+    skip = skip_ref[head]
+    row_id = lax.broadcasted_iota(jnp.int32, (CHUNK, CHUNK), 0)
+    col_id = lax.broadcasted_iota(jnp.int32, (CHUNK, CHUNK), 1)
+
+    def conv(pad, taps, i):
+        piece = pad[pl.ds(pl.multiple_of(i * CHUNK, CHUNK), CHUNK + rim), :]
+        result = taps[0:1, :] * piece[rim - 3 : rim - 3 + CHUNK, :]
+        for offset in range(1, CONV):
+            result = result + taps[offset : offset + 1, :] * piece[rim - 3 + offset : rim - 3 + offset + CHUNK, :]
+        return result
+
+    def decays(i):
+        step_row = jnp.concatenate(
+            [dt_all[rows(i * 2, 8), :][0:1, :], dt_all[rows(i * 2 + 1, 8), :][0:1, :]], axis=1
+        )
+        wide = jnp.broadcast_to(step_row, (CHUNK, CHUNK))
+        step_col = jnp.sum(jnp.where(row_id == col_id, wide, 0.0), axis=1, keepdims=True)
+        cum_col = jnp.sum(jnp.where(col_id <= row_id, wide, 0.0), axis=1, keepdims=True) * rate
+        cum_row = jnp.sum(jnp.where(row_id <= col_id, step_col, 0.0), axis=0, keepdims=True) * rate
+        end = cum_row[:, CHUNK - 1 :]
+        return step_row, step_col, cum_row, cum_col, end
+
+    def forward(i, state):
+        at = rows(i, CHUNK)
+        x_pre = conv(x_pad, taps_x, i)
+        gate = 1.0 / (1.0 + jnp.exp(-x_pre))
+        x = x_pre * gate
+        slope_all[at, :] = gate * (1.0 + x_pre * (1.0 - gate))
+        b = silu(conv(b_pad, taps_b, i))
+        c = silu(conv(c_pad, taps_c, i))
+        step_row, step_col, cum_row, cum_col, end = decays(i)
+        within = jnp.exp(jnp.where(row_id >= col_id, cum_col - cum_row, negative))
+        mix = dot3(c, b, NT) * within * step_row
+        grown = c * jnp.exp(cum_col)
+        fed = b * (jnp.exp(end - cum_col) * step_col)
+        b_all[at, :] = b
+        c_all[at, :] = c
+        y = dot3(jnp.concatenate([mix, grown], axis=1), jnp.concatenate([x, state], axis=0), NN)
+        y = y + skip * x
+        y_all[at, :] = y
+        y_ref[at, :] = y.astype(bf16)
+        return jnp.exp(end) * state + dot3(fed, x, TN)
+
+    lax.fori_loop(0, count, forward, jnp.zeros((HD, HD), f32))
+
+    def backward(k, carry):
+        state, later = carry
+        i = count - 1 - k
+        at = rows(i, CHUNK)
+        up = (y_all[at, :] - target_ref[at, :]) * (2.0 / (HEAD_TOTAL * HD))
+        b, c = b_all[at, :], c_all[at, :]
+        step_row, step_col, cum_row, cum_col, end = decays(i)
+        within = jnp.exp(jnp.where(row_id <= col_id, cum_row - cum_col, negative))
+        mix = dot3(b, c, NT) * within * step_col
+        grown = c * jnp.exp(cum_col)
+        fed = b * (jnp.exp(end - cum_col) * step_col)
+        dx = dot3(jnp.concatenate([mix, fed], axis=1), jnp.concatenate([up, state], axis=0), NN)
+        pre_grad = (dx + skip * up) * slope_all[at, :]
+        piece = jnp.concatenate([pre_grad, later], axis=0)
+        result = taps_x[0:1, :] * piece[3 : 3 + CHUNK, :]
+        for offset in range(1, CONV):
+            result = result + taps_x[offset : offset + 1, :] * piece[3 - offset : 3 - offset + CHUNK, :]
+        grad_ref[at, :] = result
+        return jnp.exp(end) * state + dot3(grown, up, TN), pre_grad[:rim, :]
+
+    lax.fori_loop(0, count, backward, (jnp.zeros((HD, HD), f32), jnp.zeros((rim, HD), f32)))
+
+
+def weight_kernel(where_ref, h_ref, *refs):
+    g_refs, out_ref = refs[:-1], refs[-1]
+    z_mine, place = where_ref[0], where_ref[1]
+    quarter = h_ref.shape[0] // 4
+    for dz in range(4):
+        total = jnp.zeros((h_ref.shape[1], HD), f32)
+        for de in range(4):
+            total = total + lax.dot_general(
+                h_ref[rows(place ^ de, quarter), :], g_refs[de][dz], TN, preferred_element_type=f32
+            )
+        out_ref[:, pl.ds(pl.multiple_of((z_mine ^ dz) * HD, HD), HD)] = total
+
+
+def head_local(
+    query_proj,
+    keyval_proj,
+    hidden,
+    weight_x,
+    conv_x,
+    conv_b,
+    conv_c,
+    step_size,
+    decay_log,
+    skip_gain,
+):
+    groups = KV // lax.axis_size("mp")
+    per_group = HEAD_TOTAL // KV
+    heads = groups * per_group
+    ctx = ("z", "x", "k")
+    z, x, k, m = (lax.axis_index(name) for name in ("z", "x", "k", "mp"))
+    place = 2 * x + k
+    where = jnp.stack([z, place, z * 4 + place]).astype(jnp.int32)
+    raw = query_proj.shape[0]
+    block = hidden.shape[0]
+    tokens = block * heads
+    half = hidden.shape[1]
+    mp = lax.axis_size("mp")
+
+    hidden_other = swap(hidden, "mp")
+    first = m == 0
+    hidden_whole = jnp.concatenate(
+        [jnp.where(first, hidden, hidden_other), jnp.where(first, hidden_other, hidden)], axis=1
+    )
+    q = query_proj.reshape(raw, mp, heads, HD).transpose(2, 1, 0, 3).reshape(mp * heads, raw, HD)
+    q = lax.all_to_all(q, ctx + ("mp",), split_axis=0, concat_axis=0, tiled=True).reshape(tokens, HD)
+    kv = keyval_proj.reshape(raw, mp, groups, 2 * HD).transpose(2, 1, 0, 3).reshape(KV, raw, 2 * HD)
+    kv = lax.all_to_all(kv, ("z", "mp"), split_axis=0, concat_axis=0, tiled=True)
+    kv_0 = kv.reshape(KV * raw, 2 * HD)
+    kv_2 = swap(kv_0, "x")
+    kv_1, kv_3 = swap(kv_0, "k"), swap(kv_2, "k")
+    kvs = (kv_0, kv_1, kv_2, kv_3)
+
+    x_input = jnp.dot(hidden_whole, weight_x, preferred_element_type=f32).astype(bf16)
+    x_send = x_input.reshape(block, groups, HD).transpose(1, 0, 2)
+    step = step_size.T.reshape(groups, 1, per_group, block)
+    high = lax.reduce_precision(step, 8, 7)
+    middle = lax.reduce_precision(step - high, 8, 7)
+    low = step - high - middle
+    pieces = jnp.concatenate([high, middle, low, jnp.zeros_like(low)], axis=1)
+    pieces = pieces.reshape(groups, 4 * per_group, block).astype(bf16)
+    x_send = jnp.concatenate([x_send, pieces], axis=1)
+    x_0 = lax.all_to_all(x_send, "z", split_axis=0, concat_axis=0, tiled=True)
+    x_2 = swap(x_0, "x")
+    x_1, x_3 = swap(x_0, "k"), swap(x_2, "k")
+    xs = (x_0, x_1, x_2, x_3)
+
+    h_part = lax.dynamic_slice_in_dim(hidden_whole, m * raw, raw, 0)
+    h_part = h_part.reshape(raw, heads, mp * half // heads).transpose(1, 0, 2)
+    h_part = lax.all_to_all(h_part, ctx, split_axis=0, concat_axis=0, tiled=True)
+    h_other = swap(h_part, "mp")
+    h_cols = jnp.stack(
+        [jnp.where(first, h_part, h_other), jnp.where(first, h_other, h_part)], axis=1
+    ).reshape(tokens, h_part.shape[2])
+
+    target = pl.pallas_call(
+        attend_kernel,
+        out_shape=jax.ShapeDtypeStruct((tokens, HD), f32),
+        in_specs=[SMEM_BLOCK] + [VMEM_BLOCK] * 5,
+        out_specs=VMEM_BLOCK,
+        scratch_shapes=[pltpu.VMEM((tokens, 2 * HD), bf16)],
+        compiler_params=PARAMS,
+        cost_estimate=pl.CostEstimate(
+            flops=2 * tokens * tokens * HD, transcendentals=tokens * tokens // 2, bytes_accessed=tokens * HD * 12
+        ),
+        name="attend",
+    )(where, q, *kvs)
+    scratch = lambda pad=0: pltpu.VMEM((tokens + pad, HD), f32)
+    y, grad = pl.pallas_call(
+        student_kernel,
+        out_shape=(jax.ShapeDtypeStruct((tokens, HD), bf16), jax.ShapeDtypeStruct((tokens, HD), f32)),
+        in_specs=[SMEM_BLOCK] * 3 + [VMEM_BLOCK] * 13,
+        out_specs=(VMEM_BLOCK, VMEM_BLOCK),
+        scratch_shapes=[scratch(8), scratch(8), scratch(8)]
+        + [scratch() for _ in range(4)]
+        + [pltpu.VMEM((16 * 8, HD), f32)],
+        compiler_params=PARAMS,
+        cost_estimate=pl.CostEstimate(
+            flops=24 * tokens * CHUNK * HD, transcendentals=tokens * CHUNK, bytes_accessed=tokens * HD * 20
+        ),
+        name="student",
+    )(where, decay_log, skip_gain, q, target, conv_x, conv_b, conv_c, *kvs, *xs)
+
+    out = lax.all_to_all(y.reshape(heads, block, HD), ctx, split_axis=0, concat_axis=0, tiled=True)
+    student_out = out.transpose(1, 0, 2).reshape(block, heads * HD)
+
+    grad = grad.reshape(2, 2, tokens // 4, HD)
+    pick = lambda array, index, axis: lax.dynamic_index_in_dim(array, index, axis, keepdims=False)
+    grad = pick(grad, k, 1) + swap(pick(grad, 1 - k, 1), "k")
+    grad = pick(grad, x, 0) + swap(pick(grad, 1 - x, 0), "x")
+    rounded = grad.astype(bf16)
+    spread = [rounded] + [
+        lax.ppermute(rounded, "z", [(i, i ^ d) for i in range(groups)]) for d in range(1, groups)
+    ]
+    g_0 = jnp.stack(spread)
+    g_2 = swap(g_0, "x")
+    g_1, g_3 = swap(g_0, "k"), swap(g_2, "k")
+    weight_grad = pl.pallas_call(
+        weight_kernel,
+        out_shape=jax.ShapeDtypeStruct((h_cols.shape[1], groups * HD), f32),
+        in_specs=[SMEM_BLOCK] + [VMEM_BLOCK] * 5,
+        out_specs=VMEM_BLOCK,
+        compiler_params=PARAMS,
+        name="weight",
+    )(where, h_cols, g_0, g_1, g_2, g_3)
+    return (student_out, weight_grad)
+
+
 def solution(mesh):
+    ctx, mp = mesh.shape["ctx"], mesh.shape["mp"]
+    groups, per_group = KV // mp, HEAD_TOTAL // KV
+    by_head = ctx == groups * per_group and per_group == 4 and groups == 4 and mp == 2
+    if by_head:
+        mesh = Mesh(mesh.devices.reshape(groups, 2, 2, mp), ("z", "x", "k", "mp"))
+        local, rows_axes = head_local, ("z", "x", "k")
+    else:
+        local, rows_axes = sequence_local, ("ctx",)
+    both = rows_axes + ("mp",)
     return jax.shard_map(
         local,
         mesh=mesh,
         in_specs=(
-            P(("ctx", "mp"), None),
-            P(("ctx", "mp"), None, None),
-            P("ctx", "mp"),
+            P(both, None),
+            P(both, None, None),
+            P(rows_axes, "mp"),
             P(None, "mp"),
             P(None, "mp"),
             P(None, "mp"),
             P(None, "mp"),
-            P("ctx", "mp"),
+            P(rows_axes, "mp"),
             P("mp"),
             P("mp"),
         ),
-        out_specs=(P("ctx", "mp"), P("ctx", "mp")),
+        out_specs=(P(rows_axes, "mp"), P(rows_axes, "mp")),
         check_vma=False,
     )

time: 539 us -> 160 us (0.30)
  waiting for transfers between devices: 318 us -> 73.8 us
  other arithmetic: 63.9 us -> 3.53 us
  matrix products: 53.1 us -> 2.9 us
  blocking collectives: 33.8 us -> 0 us
  starting transfers between devices: 6.56 us -> 39 us
  Pallas kernels: 0 us -> 28.2 us
  local copies, waits for them, and re-layouts: 35.1 us -> 10.4 us
  between operations: 14.9 us -> 0.89 us
  loops' own time: 11 us -> 0 us
    all_gather x4 -> x0, waiting for transfers between devices: 199 us -> none  [the longest x2 185 us: carried_in(): pieces = jax.tree.map(lambda part: lax.all_gather(part, axis), value)]
    reduce_scatter x1 -> x0, waiting for transfers between devices: 103 us -> none  [local(): lax.psum_scatter(lax.dot_general(hidden_whole, input_rounded, (((0,), (0,...]
    ppermute x2 -> x16, waiting for transfers between devices: 2.57 us -> 56.8 us  [the longest x13 34.8 us: swap(): return lax.ppermute(value, axis, SWAP)]
    dot_general x17 -> x1, matrix products: 53.1 us -> 2.9 us  [head_local(): jnp.dot(hidden_whole, weight_x, preferred_element_type=f32).astype(bf16)]
    select_n x30 -> x1, other arithmetic: 43.9 us -> 1.11 us  [head_local(): jnp.where(first, hidden, hidden_other)]
    pallas_call x0 -> x3, Pallas kernels: none -> 28.2 us  [the longest x1 17.1 us: head_local(): pl.pallas_call(student_kernel, out_shape=(jax.ShapeDtypeStruct((tokens, H...]
    all_gather x1 -> x0, blocking collectives: 24.6 us -> none  [carried_in(): pieces = jax.tree.map(lambda part: lax.all_gather(part, axis), value)]
    all_to_all x1 -> x5, starting transfers between devices: 3.49 us -> 23.6 us  [the longest x1 5.44 us: head_local(): x_0 = lax.all_to_all(x_send, 'z', split_axis=0, concat_axis=0, tiled=True)]
  transfers between devices with their start and end apart: 8 -> 21, of which waited for: 8 -> 9; matrix products, arithmetic and copies ran while one was open for 14% -> 8% of each run, Pallas kernels for 0% -> 5%
where the time goes in v1:
time: 160 us; the launch traced here: 159 us
  waiting for transfers between devices  73.8 us (46%)
  starting transfers between devices  39 us (24%)
  Pallas kernels  28.2 us (18%)
  local copies, waits for them, and re-layouts  10.4 us (6%)
  other arithmetic  3.53 us (2%)
  matrix products  2.9 us (2%)
    ppermute x13, waiting for transfers between devices, swap(): return lax.ppermute(value, axis, SWAP)  34.8 us
    ppermute x3, waiting for transfers between devices, head_local(): lax.ppermute(rounded, 'z', [(i, i ^ d) for i in range(groups)])  22 us
    pallas_call x1, Pallas kernels, head_local(): pl.pallas_call(student_kernel, out_shape=(jax.ShapeDtypeStruct((tokens, H...  17.1 us
    all_to_all x1, waiting for transfers between devices, head_local(): lax.all_to_all(h_part, ctx, split_axis=0, concat_axis=0, tiled=True)  12.2 us
    ppermute x13, starting transfers between devices, swap(): return lax.ppermute(value, axis, SWAP)  11 us
    pallas_call x1, Pallas kernels, head_local(): pl.pallas_call(attend_kernel, out_shape=jax.ShapeDtypeStruct((tokens, HD)...  7.16 us
    all_to_all x1, starting transfers between devices, head_local(): x_0 = lax.all_to_all(x_send, 'z', split_axis=0, concat_axis=0, tiled=True)  5.44 us
    all_to_all x1, starting transfers between devices, head_local(): lax.all_to_all(h_part, ctx, split_axis=0, concat_axis=0, tiled=True)  5.23 us
  transfers between devices with their start and end apart: 21, of which 9 were waited for; matrix products, arithmetic and copies ran while one was open for 8% of the time, Pallas kernels for 5%

profile of v1, /device:TPU:0, one launch (start us, length us, event | category | flops | bytes accessed | tf_op | source)
XLA Modules:
  0.0 158.8 jit_solution(8938945323196769880)
XLA Ops:
  0.6 3.1 %collective-permute-start.3 = (bf16[128,2048]{1,0:T(8,128)(2,1)}, bf16[128,2048]{1,0:T(8,128)(2,1)S(1)}, u32[]{:S(2)}, u32[]{:S(2)}) collective-permute-start(bf16[128,2048]{1,0:T(8,128)(2,1)} %param.12), channel_id=1, source_target_pairs={{0,1},{1,0},{2,3},{3,2},{4,5},{5,4},{6,7},{7,6},{8,9},{9,8},{10,11... | collective-permute-start | bytes 1572872 | tf_op jit(solution)/shard_map/ppermute | solution.py:251
  5.5 4.9 %all-to-all-start.1 = ((bf16[8,64,256]{2,1,0:T(8,128)(2,1)}), bf16[8,64,256]{2,1,0:T(8,128)(2,1)S(1)}, u32[]{:S(2)}, u32[]{:S(2)}) async-start(bf16[8,64,256]{2,1,0:T(8,128)(2,1)} %bitcast.7), calls=%async_computation.1 | async-start | bytes 524288 | tf_op jit(solution)/shard_map/all_to_all | solution.py:451
  11.2 6.7 %collective-permute-done.3 = bf16[128,2048]{1,0:T(8,128)(2,1)S(1)} collective-permute-done((bf16[128,2048]{1,0:T(8,128)(2,1)}, bf16[128,2048]{1,0:T(8,128)(2,1)S(1)}, u32[]{:S(2)}, u32[]{:S(2)}) %collective-permute-start.3) | collective-permute-done | bytes 524320 | tf_op jit(solution)/shard_map/ppermute | solution.py:251
  19.0 2.9 %convolution_convert_fusion = bf16[128,512]{1,0:T(8,128)(2,1)S(1)} fusion(bf16[4096,512]{1,0:T(8,128)(2,1)} %param.13, bf16[128,2048]{1,0:T(8,128)(2,1)S(1)} %get-tuple-element.9, bf16[128,2048]{1,0:T(8,128)(2,1)S(1)} %get-tuple-element.8), kind=kOutput, calls=%fused_computation.3 | convolution fusion | flops 539033600 | bytes 5373952 | tf_op jit(solution)/shard_map/dot_general | solution.py:457
  22.9 5.4 %all-to-all-start.2 = ((bf16[4,144,128]{2,1,0:T(8,128)(2,1)}), bf16[4,144,128]{2,1,0:T(8,128)(2,1)S(1)}, u32[]{:S(2)}, u32[]{:S(2)}) async-start(bf16[4,144,128]{2,1,0:T(8,128)(2,1)} %pad_maximum_fusion.4), calls=%async_computation.2 | async-start | bytes 294912 | tf_op jit(solution)/shard_map/all_to_all | solution.py:466
  29.5 4.9 %all-to-all-done.2.refs_4_ = bf16[4,144,128]{2,1,0:T(8,128)(2,1)S(1)} async-done(((bf16[4,144,128]{2,1,0:T(8,128)(2,1)}), bf16[4,144,128]{2,1,0:T(8,128)(2,1)S(1)}, u32[]{:S(2)}, u32[]{:S(2)}) %all-to-all-start.2) | async-done | bytes 147488 | tf_op jit(solution)/shard_map/all_to_all | solution.py:466
  34.3 3.8 %all-to-all-start = ((bf16[32,64,128]{2,1,0:T(8,128)(2,1)}), bf16[32,64,128]{2,1,0:T(8,128)(2,1)S(1)}, u32[]{:S(2)}, u32[]{:S(2)}) async-start(bf16[32,64,128]{2,1,0:T(8,128)(2,1)} %bitcast.4), calls=%async_computation | async-start | bytes 1048576 | tf_op jit(solution)/shard_map/all_to_all | solution.py:449
  38.2 1.8 %collective-permute-start.1 = (bf16[512,256]{1,0:T(8,128)(2,1)S(1)}, bf16[512,256]{1,0:T(8,128)(2,1)S(1)}, u32[]{:S(2)}, u32[]{:S(2)}) collective-permute-start(bf16[512,256]{1,0:T(8,128)(2,1)S(1)} %bitcast.68), channel_id=1, source_target_pairs={{0,4},{4,0},{1,5},{5,1},{2,6},{6,2},{3,7},{7,3},{8,12},{12,8},{9,1... | collective-permute-start | bytes 786440 | tf_op jit(solution)/shard_map/ppermute | solution.py:251
  40.0 11.7 %collective-permute-done.1.refs_2_ = bf16[512,256]{1,0:T(8,128)(2,1)S(1)} collective-permute-done((bf16[512,256]{1,0:T(8,128)(2,1)S(1)}, bf16[512,256]{1,0:T(8,128)(2,1)S(1)}, u32[]{:S(2)}, u32[]{:S(2)}) %collective-permute-start.1) | collective-permute-done | bytes 262176 | tf_op jit(solution)/shard_map/ppermute | solution.py:251
  52.2 5.7 %collective-permute-done.5.refs_6_ = bf16[4,144,128]{2,1,0:T(8,128)(2,1)S(1)} collective-permute-done((bf16[4,144,128]{2,1,0:T(8,128)(2,1)S(1)}, bf16[4,144,128]{2,1,0:T(8,128)(2,1)S(1)}, u32[]{:S(2)}, u32[]{:S(2)}) %collective-permute-start.5) | collective-permute-done | bytes 147488 | tf_op jit(solution)/shard_map/ppermute | solution.py:251
  59.5 7.2 %attend.1.target_ref = f32[2048,128]{1,0:T(8,128)} custom-call(s32[3]{0:T(128)} %pad_add_fusion.where_ref, bf16[2048,128]{1,0:T(8,128)(2,1)} %bitcast.63, bf16[512,256]{1,0:T(8,128)(2,1)} %bitcast.70, bf16[512,256]{1,0:T(8,128)(2,1)} %copy-done.9, bf16[512,256]{1,0:T(8,128)(2,1)} %copy-done.8, bf16[512,256]{1,0:T(8,128)(2,1)} %copy-done.10), custom_call_target="tpu_custom_call" | custom-call | flops 1073741824 | bytes 3145728 | tf_op jit(solution)/shard_map/attend/pallas_call | solution.py:479
  68.0 17.1 %student.1 = (bf16[2048,128]{1,0:T(8,128)(2,1)}, f32[2048,128]{1,0:T(8,128)}) custom-call(s32[3]{0:T(128)} %pad_add_fusion.where_ref, f32[16]{0:T(128)} %rate_ref.1, f32[16]{0:T(128)} %skip_ref.1, bf16[2048,128]{1,0:T(8,128)(2,1)} %bitcast.64, f32[2048,128]{1,0:T(8,128)} %attend.1.target_ref, f32[4,512]{1,0:T(4,128)} %conv_x_ref.1, f32[4,512]{1,0:T(4,128)} %conv_b_ref.1, ...), custom_call_target="tpu_custom_call" | custom-call | flops 1610612736 | bytes 5242880 | tf_op jit(solution)/shard_map/student/pallas_call | solution.py:492
  85.1 1.2 dynamic-slice_bitcast_fusion
  87.9 5.2 %all-to-all-start.4 = ((bf16[16,64,256]{2,1,0:T(8,128)(2,1)}), bf16[16,64,256]{2,1,0:T(8,128)(2,1)S(1)}, u32[]{:S(2)}, u32[]{:S(2)}) async-start(bf16[16,64,256]{2,1,0:T(8,128)(2,1)} %copy.33), calls=%async_computation.4 | async-start | bytes 1048576 | tf_op jit(solution)/shard_map/all_to_all | solution.py:473
  93.3 2.0 %collective-permute-start.9 = (f32[512,128]{1,0:T(8,128)S(1)}, f32[512,128]{1,0:T(8,128)S(1)}, u32[]{:S(2)}, u32[]{:S(2)}) collective-permute-start(f32[512,128]{1,0:T(8,128)S(1)} %dynamic-slice_bitcast_fusion.1), channel_id=1, source_target_pairs={{0,4},{4,0},{1,5},{5,1},{2,6},{6,2},{3,7},{7,3},{8,12},{12,8},{9,1... | collective-permute-start | bytes 786440 | tf_op jit(solution)/shard_map/ppermute | solution.py:251
  95.3 12.2 %all-to-all-done.4 = bf16[16,64,256]{2,1,0:T(8,128)(2,1)S(1)} async-done(((bf16[16,64,256]{2,1,0:T(8,128)(2,1)}), bf16[16,64,256]{2,1,0:T(8,128)(2,1)S(1)}, u32[]{:S(2)}, u32[]{:S(2)}) %all-to-all-start.4) | async-done | bytes 524320 | tf_op jit(solution)/shard_map/all_to_all | solution.py:473
  107.4 4.2 %all-to-all-start.3 = ((bf16[16,128,128]{2,1,0:T(8,128)(2,1)}), bf16[16,128,128]{2,1,0:T(8,128)(2,1)S(1)}, u32[]{:S(2)}, u32[]{:S(2)}) async-start(bf16[16,128,128]{2,1,0:T(8,128)(2,1)} %bitcast.17), calls=%async_computation.3 | async-start | bytes 1048576 | tf_op jit(solution)/shard_map/all_to_all | solution.py:507
  111.6 3.8 %collective-permute-start.12 = (bf16[512,128]{1,0:T(8,128)(2,1)S(1)}, bf16[512,128]{1,0:T(8,128)(2,1)S(1)}, u32[]{:S(2)}, u32[]{:S(2)}) collective-permute-start(bf16[512,128]{1,0:T(8,128)(2,1)S(1)} %fusion.1), channel_id=1, source_target_pairs={{0,24},{8,16},{16,8},{24,0},{1,25},{9,17},{17,9},{25,1},{2,26},{10... | collective-permute-start | bytes 393224 | tf_op jit(solution)/shard_map/ppermute | solution.py:516
  116.1 12.2 %collective-permute-done.12 = bf16[512,128]{1,0:T(8,128)(2,1)S(1)} collective-permute-done((bf16[512,128]{1,0:T(8,128)(2,1)S(1)}, bf16[512,128]{1,0:T(8,128)(2,1)S(1)}, u32[]{:S(2)}, u32[]{:S(2)}) %collective-permute-start.12) | collective-permute-done | bytes 131104 | tf_op jit(solution)/shard_map/ppermute | solution.py:516
  128.3 9.7 %collective-permute-done.11 = bf16[512,128]{1,0:T(8,128)(2,1)S(1)} collective-permute-done((bf16[512,128]{1,0:T(8,128)(2,1)S(1)}, bf16[512,128]{1,0:T(8,128)(2,1)S(1)}, u32[]{:S(2)}, u32[]{:S(2)}) %collective-permute-start.11) | collective-permute-done | bytes 131104 | tf_op jit(solution)/shard_map/ppermute | solution.py:516
  138.1 1.5 collective-permute-start.14
  139.7 1.5 collective-permute-start.7
  141.2 10.4 %collective-permute-done.14.refs_2_ = bf16[4,512,128]{2,1,0:T(8,128)(2,1)S(1)} collective-permute-done((bf16[4,512,128]{2,1,0:T(8,128)(2,1)S(1)}, bf16[4,512,128]{2,1,0:T(8,128)(2,1)S(1)}, u32[]{:S(2)}, u32[]{:S(2)}) %collective-permute-start.14) | collective-permute-done | bytes 524320 | tf_op jit(solution)/shard_map/ppermute | solution.py:251
  154.8 3.9 %weight.1 = f32[256,512]{1,0:T(8,128)} custom-call(s32[3]{0:T(128)} %pad_add_fusion.where_ref, bf16[2048,256]{1,0:T(8,128)(2,1)} %bitcast.55, bf16[4,512,128]{2,1,0:T(8,128)(2,1)} %copy-done, bf16[4,512,128]{2,1,0:T(8,128)(2,1)} %copy-done.5, bf16[4,512,128]{2,1,0:T(8,128)(2,1)} %copy-done.4, bf16[4,512,128]{2,1,0:T(8,128)(2,1)} %collective-permute-done.15.refs_3_), custom_call_target="tpu_custom_call" | custom-call | tf_op jit(solution)/shard_map/weight/pallas_call | solution.py:521
  (74 shorter events, 14.8 us)
Async XLA Ops:
  0.6 17.3 %collective-permute-start.3 = (bf16[128,2048]{1,0:T(8,128)(2,1)}, bf16[128,2048]{1,0:T(8,128)(2,1)S(1)}, u32[]{:S(2)}, u32[]{:S(2)}) collective-permute-start(bf16[128,2048]{1,0:T(8,128)(2,1)} %param.12), channel_id=1, source_target_pairs={{0,1},{1,0},{2,3},{3,2},{4,5},{5,4},{6,7},{7,6},{8,9},{9,8},{10,11... | collective-permute-start | bytes 1572872 | tf_op jit(solution)/shard_map/ppermute | solution.py:251
  5.5 17.4 %all-to-all-start.1 = ((bf16[8,64,256]{2,1,0:T(8,128)(2,1)}), bf16[8,64,256]{2,1,0:T(8,128)(2,1)S(1)}, u32[]{:S(2)}, u32[]{:S(2)}) async-start(bf16[8,64,256]{2,1,0:T(8,128)(2,1)} %bitcast.7), calls=%async_computation.1 | async-start | bytes 524288 | tf_op jit(solution)/shard_map/all_to_all | solution.py:451
  11.2 17.2 %copy-start.2 = (bf16[64,4096]{1,0:T(8,128)(2,1)S(1)}, bf16[64,4096]{1,0:T(8,128)(2,1)}, u32[]{:S(2)}) copy-start(bf16[64,4096]{1,0:T(8,128)(2,1)} %param.10) | copy-start | bytes 1572868
  22.9 35.7 %copy-start.6 = (bf16[8,64,256]{2,1,0:T(8,128)(2,1)}, bf16[8,64,256]{2,1,0:T(8,128)(2,1)S(1)}, u32[]{:S(2)}) copy-start(bf16[8,64,256]{2,1,0:T(8,128)(2,1)S(1)} %all-to-all-done.1) | copy-start | bytes 786436
  22.9 11.4 %all-to-all-start.2 = ((bf16[4,144,128]{2,1,0:T(8,128)(2,1)}), bf16[4,144,128]{2,1,0:T(8,128)(2,1)S(1)}, u32[]{:S(2)}, u32[]{:S(2)}) async-start(bf16[4,144,128]{2,1,0:T(8,128)(2,1)} %pad_maximum_fusion.4), calls=%async_computation.2 | async-start | bytes 294912 | tf_op jit(solution)/shard_map/all_to_all | solution.py:466
  34.3 32.4 %copy-start.7 = (bf16[4,144,128]{2,1,0:T(8,128)(2,1)}, bf16[4,144,128]{2,1,0:T(8,128)(2,1)S(1)}, u32[]{:S(2)}) copy-start(bf16[4,144,128]{2,1,0:T(8,128)(2,1)S(1)} %all-to-all-done.2.refs_4_) | copy-start | bytes 442372
  34.3 24.3 %all-to-all-start = ((bf16[32,64,128]{2,1,0:T(8,128)(2,1)}), bf16[32,64,128]{2,1,0:T(8,128)(2,1)S(1)}, u32[]{:S(2)}, u32[]{:S(2)}) async-start(bf16[32,64,128]{2,1,0:T(8,128)(2,1)} %bitcast.4), calls=%async_computation | async-start | bytes 1048576 | tf_op jit(solution)/shard_map/all_to_all | solution.py:449
  38.2 13.5 %collective-permute-start.1 = (bf16[512,256]{1,0:T(8,128)(2,1)S(1)}, bf16[512,256]{1,0:T(8,128)(2,1)S(1)}, u32[]{:S(2)}, u32[]{:S(2)}) collective-permute-start(bf16[512,256]{1,0:T(8,128)(2,1)S(1)} %bitcast.68), channel_id=1, source_target_pairs={{0,4},{4,0},{1,5},{5,1},{2,6},{6,2},{3,7},{7,3},{8,12},{12,8},{9,1... | collective-permute-start | bytes 786440 | tf_op jit(solution)/shard_map/ppermute | solution.py:251
  40.0 18.6 %collective-permute-start = (bf16[512,256]{1,0:T(8,128)(2,1)S(1)}, bf16[512,256]{1,0:T(8,128)(2,1)S(1)}, u32[]{:S(2)}, u32[]{:S(2)}) collective-permute-start(bf16[512,256]{1,0:T(8,128)(2,1)S(1)} %bitcast.69), channel_id=1, source_target_pairs={{0,2},{2,0},{1,3},{3,1},{4,6},{6,4},{5,7},{7,5},{8,10},{10,8},{9,1... | collective-permute-start | bytes 786440 | tf_op jit(solution)/shard_map/ppermute | solution.py:251
  51.7 6.9 %collective-permute-start.2 = (bf16[512,256]{1,0:T(8,128)(2,1)S(1)}, bf16[512,256]{1,0:T(8,128)(2,1)S(1)}, u32[]{:S(2)}, u32[]{:S(2)}) collective-permute-start(bf16[512,256]{1,0:T(8,128)(2,1)S(1)} %collective-permute-done.1.refs_2_), channel_id=1, source_target_pairs={{0,2},{2,0},{1,3},{3,1},{4,6},{6,4},{5,7},{7,5},{8,10},{10,8},{9,1... | collective-permute-start | bytes 786440 | tf_op jit(solution)/shard_map/ppermute | solution.py:251
  51.7 6.3 %collective-permute-start.5 = (bf16[4,144,128]{2,1,0:T(8,128)(2,1)S(1)}, bf16[4,144,128]{2,1,0:T(8,128)(2,1)S(1)}, u32[]{:S(2)}, u32[]{:S(2)}) collective-permute-start(bf16[4,144,128]{2,1,0:T(8,128)(2,1)S(1)} %all-to-all-done.2.refs_4_), channel_id=1, source_target_pairs={{0,4},{4,0},{1,5},{5,1},{2,6},{6,2},{3,7},{7,3},{8,12},{12,8},{9,1... | collective-permute-start | bytes 442376 | tf_op jit(solution)/shard_map/ppermute | solution.py:251
  51.8 14.9 %collective-permute-start.4 = (bf16[4,144,128]{2,1,0:T(8,128)(2,1)S(1)}, bf16[4,144,128]{2,1,0:T(8,128)(2,1)S(1)}, u32[]{:S(2)}, u32[]{:S(2)}) collective-permute-start(bf16[4,144,128]{2,1,0:T(8,128)(2,1)S(1)} %all-to-all-done.2.refs_4_), channel_id=1, source_target_pairs={{0,2},{2,0},{1,3},{3,1},{4,6},{6,4},{5,7},{7,5},{8,10},{10,8},{9,1... | collective-permute-start | bytes 442376 | tf_op jit(solution)/shard_map/ppermute | solution.py:251
  58.0 8.7 %collective-permute-start.6 = (bf16[4,144,128]{2,1,0:T(8,128)(2,1)S(1)}, bf16[4,144,128]{2,1,0:T(8,128)(2,1)S(1)}, u32[]{:S(2)}, u32[]{:S(2)}) collective-permute-start(bf16[4,144,128]{2,1,0:T(8,128)(2,1)S(1)} %collective-permute-done.5.refs_6_), channel_id=1, source_target_pairs={{0,2},{2,0},{1,3},{3,1},{4,6},{6,4},{5,7},{7,5},{8,10},{10,8},{9,1... | collective-permute-start | bytes 442376 | tf_op jit(solution)/shard_map/ppermute | solution.py:251
  86.2 6.9 %collective-permute-start.8 = (f32[2,512,128]{2,1,0:T(8,128)S(1)}, f32[2,512,128]{2,1,0:T(8,128)S(1)}, u32[]{:S(2)}, u32[]{:S(2)}) collective-permute-start(f32[2,512,128]{2,1,0:T(8,128)S(1)} %dynamic-slice_bitcast_fusion), channel_id=1, source_target_pairs={{0,2},{2,0},{1,3},{3,1},{4,6},{6,4},{5,7},{7,5},{8,10},{10,8},{9,1... | collective-permute-start | bytes 1572872 | tf_op jit(solution)/shard_map/ppermute | solution.py:251
  87.9 19.5 %all-to-all-start.4 = ((bf16[16,64,256]{2,1,0:T(8,128)(2,1)}), bf16[16,64,256]{2,1,0:T(8,128)(2,1)S(1)}, u32[]{:S(2)}, u32[]{:S(2)}) async-start(bf16[16,64,256]{2,1,0:T(8,128)(2,1)} %copy.33), calls=%async_computation.4 | async-start | bytes 1048576 | tf_op jit(solution)/shard_map/all_to_all | solution.py:473
  93.3 18.3 %collective-permute-start.9 = (f32[512,128]{1,0:T(8,128)S(1)}, f32[512,128]{1,0:T(8,128)S(1)}, u32[]{:S(2)}, u32[]{:S(2)}) collective-permute-start(f32[512,128]{1,0:T(8,128)S(1)} %dynamic-slice_bitcast_fusion.1), channel_id=1, source_target_pairs={{0,4},{4,0},{1,5},{5,1},{2,6},{6,2},{3,7},{7,3},{8,12},{12,8},{9,1... | collective-permute-start | bytes 786440 | tf_op jit(solution)/shard_map/ppermute | solution.py:251
  107.4 44.2 %all-to-all-start.3 = ((bf16[16,128,128]{2,1,0:T(8,128)(2,1)}), bf16[16,128,128]{2,1,0:T(8,128)(2,1)S(1)}, u32[]{:S(2)}, u32[]{:S(2)}) async-start(bf16[16,128,128]{2,1,0:T(8,128)(2,1)} %bitcast.17), calls=%async_computation.3 | async-start | bytes 1048576 | tf_op jit(solution)/shard_map/all_to_all | solution.py:507
  111.6 16.7 %collective-permute-start.12 = (bf16[512,128]{1,0:T(8,128)(2,1)S(1)}, bf16[512,128]{1,0:T(8,128)(2,1)S(1)}, u32[]{:S(2)}, u32[]{:S(2)}) collective-permute-start(bf16[512,128]{1,0:T(8,128)(2,1)S(1)} %fusion.1), channel_id=1, source_target_pairs={{0,24},{8,16},{16,8},{24,0},{1,25},{9,17},{17,9},{25,1},{2,26},{10... | collective-permute-start | bytes 393224 | tf_op jit(solution)/shard_map/ppermute | solution.py:516
  115.4 22.6 %collective-permute-start.11 = (bf16[512,128]{1,0:T(8,128)(2,1)S(1)}, bf16[512,128]{1,0:T(8,128)(2,1)S(1)}, u32[]{:S(2)}, u32[]{:S(2)}) collective-permute-start(bf16[512,128]{1,0:T(8,128)(2,1)S(1)} %fusion.1), channel_id=1, source_target_pairs={{0,16},{8,24},{16,0},{24,8},{1,17},{9,25},{17,1},{25,9},{2,18},{10... | collective-permute-start | bytes 393224 | tf_op jit(solution)/shard_map/ppermute | solution.py:516
  115.4 22.6 %collective-permute-start.10 = (bf16[512,128]{1,0:T(8,128)(2,1)S(1)}, bf16[512,128]{1,0:T(8,128)(2,1)S(1)}, u32[]{:S(2)}, u32[]{:S(2)}) collective-permute-start(bf16[512,128]{1,0:T(8,128)(2,1)S(1)} %fusion.1), channel_id=1, source_target_pairs={{0,8},{8,0},{16,24},{24,16},{1,9},{9,1},{17,25},{25,17},{2,10},{10... | collective-permute-start | bytes 393224 | tf_op jit(solution)/shard_map/ppermute | solution.py:516
  138.1 13.4 %collective-permute-start.14 = (bf16[4,512,128]{2,1,0:T(8,128)(2,1)S(1)}, bf16[4,512,128]{2,1,0:T(8,128)(2,1)S(1)}, u32[]{:S(2)}, u32[]{:S(2)}) collective-permute-start(bf16[4,512,128]{2,1,0:T(8,128)(2,1)S(1)} %pad_maximum_fusion.3.refs_0_), channel_id=1, source_target_pairs={{0,4},{4,0},{1,5},{5,1},{2,6},{6,2},{3,7},{7,3},{8,12},{12,8},{9,1... | collective-permute-start | bytes 1572872 | tf_op jit(solution)/shard_map/ppermute | solution.py:251
  139.7 13.1 %collective-permute-start.7 = (bf16[16,64,256]{2,1,0:T(8,128)(2,1)S(1)}, bf16[16,64,256]{2,1,0:T(8,128)(2,1)S(1)}, u32[]{:S(2)}, u32[]{:S(2)}) collective-permute-start(bf16[16,64,256]{2,1,0:T(8,128)(2,1)S(1)} %all-to-all-done.4), channel_id=1, source_target_pairs={{0,1},{1,0},{2,3},{3,2},{4,5},{5,4},{6,7},{7,6},{8,9},{9,8},{10,11... | collective-permute-start | bytes 1572872 | tf_op jit(solution)/shard_map/ppermute | solution.py:251
  141.2 12.8 %collective-permute-start.13 = (bf16[4,512,128]{2,1,0:T(8,128)(2,1)S(1)}, bf16[4,512,128]{2,1,0:T(8,128)(2,1)S(1)}, u32[]{:S(2)}, u32[]{:S(2)}) collective-permute-start(bf16[4,512,128]{2,1,0:T(8,128)(2,1)S(1)} %pad_maximum_fusion.3.refs_0_), channel_id=1, source_target_pairs={{0,2},{2,0},{1,3},{3,1},{4,6},{6,4},{5,7},{7,5},{8,10},{10,8},{9,1... | collective-permute-start | bytes 1572872 | tf_op jit(solution)/shard_map/ppermute | solution.py:251
  151.6 2.4 %collective-permute-start.15 = (bf16[4,512,128]{2,1,0:T(8,128)(2,1)S(1)}, bf16[4,512,128]{2,1,0:T(8,128)(2,1)}, u32[]{:S(2)}, u32[]{:S(2)}) collective-permute-start(bf16[4,512,128]{2,1,0:T(8,128)(2,1)S(1)} %collective-permute-done.14.refs_2_), channel_id=1, source_target_pairs={{0,2},{2,0},{1,3},{3,1},{4,6},{6,4},{5,7},{7,5},{8,10},{10,8},{9,1... | collective-permute-start | bytes 1572872 | tf_op jit(solution)/shard_map/ppermute | solution.py:251
  (11 other events, 46.7 us)
